TPU v7x, 128 devices: a whole 4x4x4 slice. The times are simulated.
128 devices in a mesh: dp: 8 (over x, core), adapter: 16 (over z, y).
Axes of the slice: x: 4, y: 4, z: 4, core: 2. Of those that a mesh axis runs over, the one named last changes fastest.
Arguments:
- residual_input: bfloat16 [65536, 2560], P(('dp', 'adapter')), may hold values from -6 to 6
- input_norm_gain: float32 [2560], replicated, may hold values from 0.5 to 1.5
- base_projection_weight: bfloat16 [2560, 4096], P('adapter', 'dp'), may hold values from -0.125 to 0.125
- query_key_gains: float32 [2, 256], replicated, may hold values from 0.5 to 1.5
- adapter_down_weight: bfloat16 [64, 2560, 48], P('adapter'), may hold values from -0.125 to 0.125
- adapter_up_weight: bfloat16 [64, 16, 4096], P('adapter'), may hold values from -1.5 to 1.5
- row_adapter_index: int32 [65536, 1], P(('dp', 'adapter')), may hold values from 0 to 63; in each aligned block of 512 rows (0 to 511, 512 to 1023, ...) at most 16 rows name the same one
- row_sequence_index: int32 [65536], P(('dp', 'adapter')), may hold values from 0 to 7, never falling along the last dimension, each value on 1 to 12288 neighbouring positions
Outputs:
- attended: bfloat16 [65536, 2048], P(('dp', 'adapter'))
Inputs may be any that keep to these rules, and one draw needn't show every extreme that they name: `row_adapter_index`: among the rows of one device, no adapter serves more than 16 rows; some adapter serves exactly 16 rows of some device. `row_sequence_index`: sequence numbers never fall along the rows; every sequence has 1 to 12288 rows, one exactly 12288.
All inputs are finite; a program needn't handle non-finite values.
Results may differ from a plain program's by a relative error of at most 0.02.
Values may be sent and summed in bfloat16 or wider, within the bound.
A program may use at most 128 MiB of HBM per device.

v0:
```python
import jax
import jax.numpy as jnp
from jax import lax
from jax.sharding import PartitionSpec as P

HEADS = 8
KV_HEADS = 4
HEAD_DIM = 256
WINDOW = 1024


def shifted(value, axis, by):
    size = lax.axis_size(axis)
    pairs = [(i, i + by) for i in range(size) if 0 <= i + by < size]
    return lax.ppermute(value, axis, pairs)


def head_norm(block, heads, gain):
    shaped = block.reshape(block.shape[0], heads, HEAD_DIM)
    scaled = shaped * lax.rsqrt(jnp.mean(shaped * shaped, axis=-1, keepdims=True) + 1e-06) * gain
    return scaled.astype(jnp.bfloat16)


def adapter_delta(rank_values, up_matrices):
    width_q = HEADS * HEAD_DIM
    width_k = KV_HEADS * HEAD_DIM
    inner = up_matrices.shape[1]
    part_q = jnp.einsum(
        "nacr,arq->nacq",
        rank_values[..., 0:inner],
        up_matrices[:, :, 0:width_q],
        preferred_element_type=jnp.float32,
    )
    part_k = jnp.einsum(
        "nacr,arq->nacq",
        rank_values[..., inner : 2 * inner],
        up_matrices[:, :, width_q : width_q + width_k],
        preferred_element_type=jnp.float32,
    )
    part_v = jnp.einsum(
        "nacr,arq->nacq",
        rank_values[..., 2 * inner : 3 * inner],
        up_matrices[:, :, width_q + width_k :],
        preferred_element_type=jnp.float32,
    )
    return jnp.concatenate([part_q, part_k, part_v], axis=-1).astype(jnp.bfloat16)


def adapter_ranks(adapter_slots, down_matrices):
    return jnp.einsum(
        "nacd,adr->nacr", adapter_slots, down_matrices, preferred_element_type=jnp.float32
    ).astype(jnp.bfloat16)


def body(
    residual_input,
    input_norm_gain,
    base_projection_weight,
    query_key_gains,
    adapter_down_weight,
    adapter_up_weight,
    row_adapter_index,
    row_sequence_index,
):
    rows = residual_input.shape[0]
    width = residual_input.shape[1]
    width_q = HEADS * HEAD_DIM
    width_k = KV_HEADS * HEAD_DIM
    group = HEADS // KV_HEADS
    values_in = residual_input.astype(jnp.float32)
    normed = (
        values_in
        * lax.rsqrt(jnp.mean(values_in * values_in, axis=-1, keepdims=True) + 1e-06)
        * input_norm_gain
    ).astype(jnp.bfloat16)
    slab = lax.all_gather(base_projection_weight, "dp", axis=1, tiled=True)
    base = jnp.dot(
        normed,
        lax.all_gather(slab, "adapter", axis=0, tiled=True),
        preferred_element_type=jnp.float32,
    ).astype(jnp.bfloat16)
    total_width = base.shape[1]
    owners = lax.axis_size("adapter")
    local_adapter_count = adapter_down_weight.shape[0]
    adapters_all = owners * local_adapter_count
    capacity = 2 * rows // adapters_all
    adapter_ids = row_adapter_index[:, 0]
    onehot = (adapter_ids[:, None] == jnp.arange(adapters_all, dtype=jnp.int32)[None, :]).astype(
        jnp.int32
    )
    earlier = jnp.cumsum(onehot, axis=0) - onehot
    place = jnp.sum(earlier * onehot, axis=1)
    slot = adapter_ids * capacity + place
    scratch_buffer = jnp.zeros((adapters_all * capacity, width), jnp.bfloat16).at[slot].set(normed)
    scratch_buffer = scratch_buffer.reshape(owners, local_adapter_count, capacity, width)
    adapter_corrections = adapter_delta(
        adapter_ranks(
            lax.all_to_all(scratch_buffer, "adapter", split_axis=0, concat_axis=0, tiled=True),
            adapter_down_weight,
        ),
        adapter_up_weight,
    )
    returned = lax.all_to_all(
        adapter_corrections, "adapter", split_axis=0, concat_axis=0, tiled=True
    )
    delta_slots = returned.reshape(adapters_all * capacity, total_width)
    delta_update = delta_slots[slot]
    projected = base.astype(jnp.float32) + delta_update.astype(jnp.float32)
    queries = head_norm(projected[:, 0:width_q], HEADS, query_key_gains[0]).reshape(
        rows, KV_HEADS, group, HEAD_DIM
    )
    keys = head_norm(
        projected[:, width_q : width_q + width_k], KV_HEADS, query_key_gains[1]
    ).reshape(rows, width_k)
    values = projected[:, width_q + width_k :].astype(jnp.bfloat16)
    before = (WINDOW + rows - 2) // rows
    key_parts = []
    value_parts = []
    seg_parts = []
    for offset in range(before, 0, -1):
        moved_keys, moved_values, moved_seg = shifted(
            (keys, values, row_sequence_index), ("dp", "adapter"), offset
        )
        key_parts.append(moved_keys)
        value_parts.append(moved_values)
        seg_parts.append(moved_seg)
    key_parts.append(keys)
    value_parts.append(values)
    seg_parts.append(row_sequence_index)
    span = (before + 1) * rows
    key_all = jnp.concatenate(key_parts, axis=0).reshape(span, KV_HEADS, HEAD_DIM)
    value_all = jnp.concatenate(value_parts, axis=0).reshape(span, KV_HEADS, HEAD_DIM)
    seg_all = jnp.concatenate(seg_parts, axis=0)
    position = lax.axis_index(("dp", "adapter"))
    query_pos = position * rows + jnp.arange(rows, dtype=jnp.int32)
    key_pos = (position - before) * rows + jnp.arange(span, dtype=jnp.int32)
    gap = query_pos[:, None] - key_pos[None, :]
    allowed = (
        (row_sequence_index[:, None] == seg_all[None, :])
        & (gap >= 0)
        & (gap < WINDOW)
        & (key_pos[None, :] >= 0)
    )
    scores = jnp.einsum(
        "tkgd,skd->kgts", queries, key_all, preferred_element_type=jnp.float32
    ) * HEAD_DIM ** (-0.5)
    weights = jnp.where(allowed[None, None], jnp.exp(scores), jnp.float32(0.0))
    total = jnp.sum(weights, axis=-1)
    probs = weights.astype(jnp.bfloat16)
    summed = jnp.einsum("kgts,skd->tkgd", probs, value_all, preferred_element_type=jnp.float32)
    result = summed / jnp.transpose(total, (2, 0, 1))[..., None]
    return result.reshape(rows, width_q).astype(jnp.bfloat16)


def solution(mesh):
    placed = (
        P(("dp", "adapter"), None),
        P(),
        P("adapter", "dp"),
        P(),
        P("adapter", None, None),
        P("adapter", None, None),
        P(("dp", "adapter"), None),
        P(("dp", "adapter")),
    )
    return jax.shard_map(
        body, mesh=mesh, in_specs=placed, out_specs=P(("dp", "adapter"), None), check_vma=False
    )
```

profile of v0, /device:TPU:3, one launch (start us, length us, event | category | flops | bytes accessed | tf_op | source)
XLA Modules:
  0.0 495.9 jit_solution(7275896673530061145)
XLA Ops:
  6.5 0.7 all-gather.3.cloned.1.call-update
  7.3 26.8 %all-gather.3.cloned.1.call-done = bf16[160,4096]{1,0:T(8,128)(2,1)} async-done(((bf16[160,512]{1,0:T(8,128)(2,1)}), bf16[160,4096]{1,0:T(8,128)(2,1)}) %all-gather.3.cloned.1.call-update) | async-done | bytes 1310736 | tf_op jit(solution)/shard_map/all_gather | solution.py:76
  34.2 0.7 fusion.51
  34.9 1.2 reduce-window.6
  36.1 0.2 slice_reduce_fusion
  36.3 0.8 fusion.46
  37.2 2.3 fusion.7
  39.5 9.0 %scatter_custom_fusion = bf16[1024,2560]{1,0:T(8,128)(2,1)} fusion(s32[512]{0:T(512)S(1)} %bitcast.120, bf16[]{:T(256)} %constant.17.clone.1, bf16[512,2560]{1,0:T(8,128)(2,1)} %param.8, f32[2560]{0:T(1024)S(1)} %copy-done.8, f32[512]{0:T(512)S(1)} %add_rsqrt_fusion.2), kind=kCustom, calls=%fused_computation.37 | custom fusion | flops 5242880 | bytes 7878658 | tf_op jit(solution)/shard_map/scatter | solution.py:94
  48.5 83.8 %all_to_all.10 = bf16[16,4,16,2560]{3,2,1,0:T(8,128)(2,1)S(1)} all-to-all(bf16[16,4,16,2560]{3,2,1,0:T(8,128)(2,1)} %bitcast.105), channel_id=1, replica_groups=mesh['dp'=8,'adapter'=16] {'adapter'}, dimensions={0} | all-to-all | bytes 10485760 | tf_op jit(solution)/shard_map/all_to_all | solution.py:98
  132.4 1.5 fusion.33
  133.9 0.7 convert_bitcast_fusion.1
  134.6 0.7 convert_bitcast_fusion.2
  135.4 1.2 convert_bitcast_fusion
  136.6 4.3 pad_maximum_fusion
  140.9 8.3 %copy.62 = bf16[16,4,16,4096]{3,2,1,0:T(8,128)(2,1)} copy(bf16[16,4,16,4096]{3,2,0,1:T(8,128)(2,1)} %pad_maximum_fusion) | data formatting | bytes 16777216 | tf_op jit(solution)/shard_map/concatenate | solution.py:46
  149.2 5.1 %all-to-all-start.1 = ((bf16[16,4,16,4096]{3,2,1,0:T(8,128)(2,1)}), bf16[16,4,16,4096]{3,2,1,0:T(8,128)(2,1)}, u32[]{:S(2)}, u32[]{:S(2)}) async-start(bf16[16,4,16,4096]{3,2,1,0:T(8,128)(2,1)} %copy.62), calls=%async_computation.1 | async-start | bytes 16777216 | tf_op jit(solution)/shard_map/all_to_all | solution.py:103
  154.3 3.1 collective-permute-start.3
  157.4 4.3 collective-permute-start.2
  161.8 151.0 %collective-permute-done.3 = s32[512]{0:T(512)S(1)} collective-permute-done((s32[512]{0:T(512)S(1)}, s32[512]{0:T(512)S(1)}, u32[]{:S(2)}, u32[]{:S(2)}) %collective-permute-start.3) | collective-permute-done | bytes 2080 | tf_op jit(solution)/shard_map/ppermute | solution.py:15
  312.8 15.8 %collective-permute-done.2 = s32[512]{0:T(512)S(1)} collective-permute-done((s32[512]{0:T(512)S(1)}, s32[512]{0:T(512)S(1)}, u32[]{:S(2)}, u32[]{:S(2)}) %collective-permute-start.2) | collective-permute-done | bytes 2080 | tf_op jit(solution)/shard_map/ppermute | solution.py:15
  328.6 2.5 fusion.22
  331.1 13.0 %gather_fusion = bf16[512,4096]{1,0:T(8,128)(2,1)} fusion(bf16[1024,4096]{1,0:T(8,128)(2,1)} %bitcast.18, s32[1024]{0:T(1024)S(1)} %pad_clamp_fusion), kind=kCustom, calls=%fused_computation | custom fusion | bytes 8390656 | tf_op jit(solution)/shard_map/gather | solution.py:107
  344.1 16.6 %convert_add_fusion = f32[512,4096]{1,0:T(8,128)S(1)} fusion(bf16[512,4096]{1,0:T(8,128)(2,1)} %gather_fusion, bf16[2560,4096]{1,0:T(8,128)(2,1)} %all-gather.5.cloned.1.call-done, bf16[512,2560]{1,0:T(8,128)(2,1)} %param.8, f32[2560]{0:T(1024)S(1)} %copy-done.8, f32[512]{0:T(512)S(1)} %add_rsqrt_fusion.2), kind=kOutput, calls=%fused_computation.10 | convolution fusion | flops 10751049728 | bytes 36188160 | tf_op jit(solution)/shard_map/dot_general | solution.py:77
  360.7 1.3 slice.85
  362.0 1.9 collective-permute-start.1
  363.9 1.9 collective-permute-start
  365.9 1.5 slice_multiply_fusion
  367.4 2.2 mul.115
  369.6 0.6 reduce_sum.50
  370.3 0.6 mul.116
  370.9 0.5 copy.85
  371.3 2.3 multiply_convert_fusion
  373.6 2.1 collective-permute-start.5
  375.7 3.1 collective-permute-start.4
  378.9 4.3 slice_multiply_fusion.1
  383.2 6.6 %reshape.168 = f32[512,4,2,256]{3,2,1,0:T(2,128)} reshape(f32[512,2048]{1,0:T(8,128)} %get-tuple-element.6) | data formatting | bytes 8388608 | tf_op jit(solution)/shard_map/reshape | solution.py:19
  389.8 6.1 %copy.87 = f32[64,8,8,256]{3,2,1,0:T(8,128)} copy(f32[64,8,8,256]{3,1,2,0:T(8,128)} %bitcast.106) | data formatting | bytes 8388608
  395.9 2.8 reduce_sum.51
  398.8 1.0 copy.107
  399.9 36.2 %collective-permute-done.1 = bf16[512,1024]{1,0:T(8,128)(2,1)} collective-permute-done((bf16[512,1024]{1,0:T(8,128)(2,1)}, bf16[512,1024]{1,0:T(8,128)(2,1)}, u32[]{:S(2)}, u32[]{:S(2)}) %collective-permute-start.1) | collective-permute-done | bytes 1048608 | tf_op jit(solution)/shard_map/ppermute | solution.py:15
  436.1 3.2 pad_maximum_fusion.1
  439.3 4.8 copy.80
  444.0 14.5 %collective-permute-done.5 = bf16[512,1024]{1,0:T(8,128)(2,1)} collective-permute-done((bf16[512,1024]{1,0:T(8,128)(2,1)S(1)}, bf16[512,1024]{1,0:T(8,128)(2,1)}, u32[]{:S(2)}, u32[]{:S(2)}) %collective-permute-start.5) | collective-permute-done | bytes 1048608 | tf_op jit(solution)/shard_map/ppermute | solution.py:15
  458.5 2.3 copy.108
  460.8 1.3 copy.109
  462.1 13.2 %fusion = (f32[4,2,512]{2,1,0:T(2,128)S(1)}, f32[4,1536,512,2]{2,1,3,0:T(8,128)}) fusion(pred[512,1536]{0,1:T(8,128)(4,1)S(1)} %copy-done.5, f32[512,4,2,256]{3,2,1,0:T(2,128)S(1)} %copy-done.4, f32[256]{0:T(256)S(1)} %bitcast.123, f32[512,4,2]{0,2,1:T(2,128)S(1)} %rsqrt.30, bf16[512,4,256]{2,0,1:T(8,128)(2,1)} %bitcast.113, ...), kind=kOutput, calls=%fused_computation.3 | convolution fusion | flops 3252678656 | bytes 33326080 | tf_op jit(solution)/shard_map/tkgd,skd->kgts/dot_general | solution.py:144
  475.3 11.4 %fusion.12 = bf16[512,4,2,256]{0,3,2,1:T(8,128)(2,1)S(1)} fusion(bf16[1536,4,256,1]{0,2,3,1:T(8,128)(2,1)} %bitcast.111, f32[4,1536,512,2]{2,1,3,0:T(8,128)} %get-tuple-element.10, pred[512,1536]{0,1:T(8,128)(4,1)} %fusion.22, f32[512,4,2]{0,2,1:T(2,128)S(1)} %bitcast.124), kind=kOutput, calls=%fused_computation.22 | convolution fusion | flops 3242196992 | bytes 31211520 | tf_op jit(solution)/shard_map/kgts,skd->tkgd/dot_general | solution.py:150
  486.7 2.4 copy.72
  (45 shorter events, 0.4 us)
Async XLA Ops:
  6.5 125.8 %copy-start = (bf16[4,2560,48]{1,2,0:T(8,128)(2,1)S(1)}, bf16[4,2560,48]{1,2,0:T(8,128)(2,1)}, u32[]{:S(2)}) copy-start(bf16[4,2560,48]{1,2,0:T(8,128)(2,1)} %param.12) | copy-start | bytes 2949124
  6.5 33.0 %copy-start.7 = (s32[512,1]{0,1:T(1,128)S(1)}, s32[512,1]{0,1:T(1,128)}, u32[]{:S(2)}) copy-start(s32[512,1]{0,1:T(1,128)} %param.14) | copy-start | bytes 6148
  6.5 33.0 %copy-start.8 = (f32[2560]{0:T(1024)S(1)}, f32[2560]{0:T(1024)}, u32[]{:S(2)}) copy-start(f32[2560]{0:T(1024)} %param.9) | copy-start | bytes 30724
  6.5 27.6 %all-gather.3.cloned.1.call-start = ((), (), s32[]{:S(2)}) async-start(), calls=%async_computation.2 | async-start | bytes 1474560 | tf_op jit(solution)/shard_map/all_gather | solution.py:76
  7.3 336.8 %all-gather.5.cloned.1.call-start = ((), (), s32[]{:S(2)}) async-start(), calls=%async_computation.3 | async-start | bytes 22282240 | tf_op jit(solution)/shard_map/all_gather | solution.py:79
  132.4 1.5 copy-start.6
  149.2 5.1 %copy-start.9 = (s32[512]{0:T(512)S(1)}, s32[512]{0:T(512)}, u32[]{:S(2)}) copy-start(s32[512]{0:T(512)} %param.15) | copy-start | bytes 6148
  149.2 12.6 %copy-start.10 = (f32[2,256]{1,0:T(2,128)S(1)}, f32[2,256]{1,0:T(2,128)}, u32[]{:S(2)}) copy-start(f32[2,256]{1,0:T(2,128)} %param.11) | copy-start | bytes 6148
  149.2 181.9 %all-to-all-start.1 = ((bf16[16,4,16,4096]{3,2,1,0:T(8,128)(2,1)}), bf16[16,4,16,4096]{3,2,1,0:T(8,128)(2,1)}, u32[]{:S(2)}, u32[]{:S(2)}) async-start(bf16[16,4,16,4096]{3,2,1,0:T(8,128)(2,1)} %copy.62), calls=%async_computation.1 | async-start | bytes 16777216 | tf_op jit(solution)/shard_map/all_to_all | solution.py:103
  154.3 158.5 %collective-permute-start.3 = (s32[512]{0:T(512)S(1)}, s32[512]{0:T(512)S(1)}, u32[]{:S(2)}, u32[]{:S(2)}) collective-permute-start(s32[512]{0:T(512)S(1)} %copy-done.9), channel_id=1, source_target_pairs={{0,1},{1,2},{2,3},{3,4},{4,5},{5,6},{6,7},{7,8},{8,9},{9,10},{10,1... | collective-permute-start | bytes 6152 | tf_op jit(solution)/shard_map/ppermute | solution.py:15
  157.4 171.2 %collective-permute-start.2 = (s32[512]{0:T(512)S(1)}, s32[512]{0:T(512)S(1)}, u32[]{:S(2)}, u32[]{:S(2)}) collective-permute-start(s32[512]{0:T(512)S(1)} %copy-done.9), channel_id=1, source_target_pairs={{0,2},{1,3},{2,4},{3,5},{4,6},{5,7},{6,8},{7,9},{8,10},{9,11},{10,... | collective-permute-start | bytes 6152 | tf_op jit(solution)/shard_map/ppermute | solution.py:15
  360.7 5.1 %copy-start.2 = (f32[512,4096]{1,0:T(8,128)}, f32[512,4096]{1,0:T(8,128)S(1)}, u32[]{:S(2)}) copy-start(f32[512,4096]{1,0:T(8,128)S(1)} %convert_add_fusion) | copy-start | bytes 25165828
  362.0 74.0 %collective-permute-start.1 = (bf16[512,1024]{1,0:T(8,128)(2,1)}, bf16[512,1024]{1,0:T(8,128)(2,1)}, u32[]{:S(2)}, u32[]{:S(2)}) collective-permute-start(bf16[512,1024]{1,0:T(8,128)(2,1)} %slice.85), channel_id=1, source_target_pairs={{0,1},{1,2},{2,3},{3,4},{4,5},{5,6},{6,7},{7,8},{8,9},{9,10},{10,1... | collective-permute-start | bytes 3145736 | tf_op jit(solution)/shard_map/ppermute | solution.py:15
  363.9 72.1 %collective-permute-start = (bf16[512,1024]{1,0:T(8,128)(2,1)}, bf16[512,1024]{1,0:T(8,128)(2,1)}, u32[]{:S(2)}, u32[]{:S(2)}) collective-permute-start(bf16[512,1024]{1,0:T(8,128)(2,1)} %slice.85), channel_id=1, source_target_pairs={{0,2},{1,3},{2,4},{3,5},{4,6},{5,7},{6,8},{7,9},{8,10},{9,11},{10,... | collective-permute-start | bytes 3145736 | tf_op jit(solution)/shard_map/ppermute | solution.py:15
  370.9 8.0 %copy-start.3 = (f32[512,4096]{1,0:T(8,128)S(1)}, f32[512,4096]{1,0:T(8,128)}, u32[]{:S(2)}) copy-start(f32[512,4096]{1,0:T(8,128)} %copy-done.2) | copy-start | bytes 25165828
  373.6 84.9 %collective-permute-start.5 = (bf16[512,1024]{1,0:T(8,128)(2,1)S(1)}, bf16[512,1024]{1,0:T(8,128)(2,1)}, u32[]{:S(2)}, u32[]{:S(2)}) collective-permute-start(bf16[512,1024]{1,0:T(8,128)(2,1)S(1)} %multiply_convert_fusion), channel_id=1, source_target_pairs={{0,1},{1,2},{2,3},{3,4},{4,5},{5,6},{6,7},{7,8},{8,9},{9,10},{10,1... | collective-permute-start | bytes 3145736 | tf_op jit(solution)/shard_map/ppermute | solution.py:15
  375.7 85.1 %collective-permute-start.4 = (bf16[512,1024]{1,0:T(8,128)(2,1)S(1)}, bf16[512,1024]{1,0:T(8,128)(2,1)}, u32[]{:S(2)}, u32[]{:S(2)}) collective-permute-start(bf16[512,1024]{1,0:T(8,128)(2,1)S(1)} %multiply_convert_fusion), channel_id=1, source_target_pairs={{0,2},{1,3},{2,4},{3,5},{4,6},{5,7},{6,8},{7,9},{8,10},{9,11},{10,... | collective-permute-start | bytes 3145736 | tf_op jit(solution)/shard_map/ppermute | solution.py:15
  439.3 22.8 %copy-start.5 = (pred[512,1536]{0,1:T(8,128)(4,1)S(1)}, pred[512,1536]{0,1:T(8,128)(4,1)}, u32[]{:S(2)}) copy-start(pred[512,1536]{0,1:T(8,128)(4,1)} %fusion.22) | copy-start | bytes 2359300
  444.0 18.1 %copy-start.4 = (f32[512,4,2,256]{3,2,1,0:T(2,128)S(1)}, f32[512,4,2,256]{3,2,1,0:T(2,128)}, u32[]{:S(2)}) copy-start(f32[512,4,2,256]{3,2,1,0:T(2,128)} %reshape.168) | copy-start | bytes 12582916
  475.3 13.8 %copy-start.1 = (bf16[4,2560,48]{1,2,0:T(8,128)(2,1)S(1)}, bf16[4,2560,48]{1,2,0:T(8,128)(2,1)}, u32[]{:S(2)}) copy-start(bf16[4,2560,48]{1,2,0:T(8,128)(2,1)} %param.12) | copy-start | bytes 2949124
Sparse Core Ops, SparseCore 0:
  9.1 25.0 all-gather.2
  36.3 278.7 all-gather.4
where the time goes:
time: 497 us; the launch traced here: 496 us
  waiting for transfers between devices  245 us (49%)
  blocking collectives  83.8 us (17%)
  local copies, waits for them, and re-layouts  50.7 us (10%)
  matrix products  45.4 us (9%)
  other arithmetic  35.7 us (7%)
  starting transfers between devices  21.5 us (4%)
  between operations  13.8 us (3%)
    ppermute x6, waiting for transfers between devices, shifted(): return lax.ppermute(value, axis, pairs)  217 us
    all_to_all x1, blocking collectives, body(): lax.all_to_all(scratch_buffer, 'adapter', split_axis=0, concat_axis=0, ti...  83.8 us
    all_gather x1, waiting for transfers between devices, body(): slab = lax.all_gather(base_projection_weight, 'dp', axis=1, tiled=True)  26.8 us
    dot_general x1, matrix products, body(): jnp.dot(normed, lax.all_gather(slab, 'adapter', axis=0, tiled=True), pref...  16.6 us
    ppermute x6, starting transfers between devices, shifted(): return lax.ppermute(value, axis, pairs)  16.4 us
    dot_general x1, matrix products, body(): jnp.einsum('tkgd,skd->kgts', queries, key_all, preferred_element_type=jnp...  13.2 us
    gather x1, local copies, waits for them, and re-layouts, body(): delta_update = delta_slots[slot]  13 us
    dot_general x1, matrix products, body(): jnp.einsum('kgts,skd->tkgd', probs, value_all, preferred_element_type=jnp...  11.4 us
  transfers between devices with their start and end apart: 9, of which 5 were waited for; matrix products, arithmetic and copies ran while one was open for 17% of the time, Pallas kernels for 0%

commit v1 on v0

v1 whole, which is shorter than its diff:
```python
import jax
import jax.numpy as jnp
import numpy as np
from jax import lax
from jax.experimental import pallas as pl
from jax.experimental.pallas import tpu as pltpu
from jax.sharding import PartitionSpec as P

HEADS = 8
KV_HEADS = 4
HEAD_DIM = 256
ROWS = 512
WIDTH = 2560
BF16 = jnp.bfloat16
F32 = jnp.float32


def dot(a, b, dims=((1,), (0,))):
    return lax.dot_general(a, b, (dims, ((), ())), preferred_element_type=F32)


def kernel(
    x_ref, g_ref, gains_ref, ids_ref, fold_ref, tile_ref, cols_ref, w_ref, d_ref, u_ref,
    out_ref,
    xg, wu, dn, rpt, qs, kall, vall, ob, ids, hids, acol, scol, krow,
    sh_send, d_sem, u_sem, w_sem, x_send, x_recv, f_send, i_send, i_recv,
    g_send, g_recv, r_send, r_recv, h_send, h_recv, o_send, o_recv,
):
    dp = lax.axis_index("dp")
    ad = lax.axis_index("adapter")
    x, c = dp // 2, dp % 2
    z, y = ad // 4, ad % 4
    g, yl = y // 2, y % 2

    def dev(x_, c_, z_, y_):
        return (x_ * 2 + c_, z_ * 4 + y_)

    def half_of(y_):
        return ((y_ + 1) // 2) % 2

    def remote(src, dst, ssem, rsem, to):
        return pltpu.make_async_remote_copy(
            src_ref=src, dst_ref=dst, send_sem=ssem, recv_sem=rsem,
            device_id=to, device_id_type=pl.DeviceIdType.MESH,
        )

    def arrived(ref, sem):
        pltpu.make_async_copy(ref, ref, sem).wait()

    half = half_of(y)
    kv = c + 2 * half
    ypar = 1 - 2 * yl + y
    sib = dev(x, 1 - c, z, y)
    mate = dev(x, c, z, ypar)
    diag = dev(x, 1 - c, z, ypar)
    xbit = x // 2
    b = (1 - xbit) * (x % 2) + xbit * c
    px = (1 - xbit) * (1 - x) + xbit * x
    pc = (1 - xbit) * c + xbit * (1 - c)
    up_x, dn_x = (x + 1) % 4, (x + 3) % 4
    up_z, dn_z = (z + 1) % 4, (z + 3) % 4
    y3 = 3 - y
    wrap = g * (z // 3)
    tz = (z + g) % 4
    swrap = (1 - g) * ((3 - z) // 3)
    sz = (z + 3 + g) % 4
    halo_to = [dev(x, c, tz, y3), dev((x + wrap) % 4, c, tz, y3)]
    halo_from = [dev((x + 4 - swrap) % 4, c, sz, y3), dev(x, c, sz, y3)]
    slot_of = [wrap, 1 - wrap]

    barrier = pltpu.get_barrier_semaphore()
    partners = [sib, mate, diag]
    partners += [dev(x, c, z, (y + k) % 4) for k in (1, 2, 3)]
    partners += [dev(px, pc, z, k) for k in range(4)]
    partners += [dev(up_x, c, z, y), dev(dn_x, c, z, y), dev(x, c, up_z, y), dev(x, c, dn_z, y)]
    partners += halo_to + halo_from
    for to in partners:
        pl.semaphore_signal(barrier, inc=1, device_id=to, device_id_type=pl.DeviceIdType.MESH)
    pl.semaphore_wait(barrier, len(partners))

    pending = []

    def go(copy):
        copy.start()
        pending.append(copy)
        return copy

    y2 = (y + 2) % 4
    dsrc = d_ref.at[pl.ds(pl.multiple_of(96 * c, 32), 96), pl.ds(pl.multiple_of(640 * x, 128), 640)]
    ddst = dn.at[z, pl.ds(pl.multiple_of(96 * g, 32), 96), pl.ds(pl.multiple_of(640 * x, 128), 640)]
    dloc = pltpu.make_async_copy(dsrc, ddst, d_sem.at[0])
    dloc.start()
    dsend = go(remote(dsrc, ddst, sh_send.at[0], d_sem.at[1], dev(x, c, z, y2)))

    def up_src(y_):
        kv_ = c + 2 * half_of(y_)
        col = (1 - xbit) * (kv_ * 512 + x * 256) + xbit * (2048 + (x - 2) * 1024 + kv_ * 256)
        return u_ref.at[:, pl.ds(pl.multiple_of(col, 128), 256)]

    udst = wu.at[x, z, pl.ds(pl.multiple_of(640 + 64 * y, 64), 64), :]
    for k in (1, 2, 3):
        yt = (y + k) % 4
        go(remote(up_src(yt), udst, sh_send.at[k], u_sem.at[y], dev(x, c, z, yt)))
    pltpu.make_async_copy(up_src(y), udst, u_sem.at[y]).start()
    kept = w_ref.at[:, pl.ds(pl.multiple_of(b * 256, 256), 256)]
    other = w_ref.at[:, pl.ds(pl.multiple_of((1 - b) * 256, 256), 256)]
    wrows = pl.ds(pl.multiple_of(160 * y, 32), 160)
    kept_sends = []
    for k, yt in enumerate((b, 3 - b)):
        send = remote(kept, wu.at[x, z, wrows, :], sh_send.at[4 + k], w_sem.at[y], dev(x, c, z, yt))
        kept_sends.append((yt, send))

        @pl.when(yt == y)
        def _():
            pltpu.make_async_copy(kept, wu.at[x, z, wrows, :], w_sem.at[y]).start()

        @pl.when(yt != y)
        def _():
            send.start()

        go(remote(other, wu.at[px, z, wrows, :], sh_send.at[6 + k], w_sem.at[y], dev(px, pc, z, yt)))

    own = 2 * c + yl
    iloc = pltpu.make_async_copy(ids_ref, ids.at[own], i_recv.at[own])
    iloc.start()
    for k, to in enumerate((sib, mate, diag)):
        go(remote(ids_ref, ids.at[own], i_send.at[k], i_recv.at[own], to))
    for k in range(4):
        val = x_ref[k * 128 : (k + 1) * 128, :].astype(F32)
        scale = lax.rsqrt(jnp.mean(val * val, axis=-1, keepdims=True) + 1e-06)
        rows = pl.ds(pl.multiple_of(own * 512 + k * 128, 128), 128)
        xg[rows, :] = (val * scale * g_ref[...]).astype(BF16)
        go(remote(xg.at[rows, :], xg.at[rows, :], x_send.at[0, k], x_recv.at[0, k], mate))
        go(remote(xg.at[rows, :], xg.at[rows, :], x_send.at[1, k], x_recv.at[1, k], sib))

    def block_rows(blk, k):
        return xg.at[pl.ds(pl.multiple_of(blk * 512 + k * 128, 128), 128), :]

    def slot(part, stage, i, lo, n):
        if part < 2:
            rows = pl.ds(part * 96 + lo, n)
            cols_i = pl.ds(pl.multiple_of(i * 640, 128), 640)
            cols_x = pl.ds(pl.multiple_of(x * 640, 128), 640)
            if part == 0:
                return dn.at[z, rows, cols_i] if stage == 0 else dn.at[i, rows, :]
            return dn.at[i, rows, cols_x] if stage == 0 else dn.at[:, rows, cols_i]
        rows = pl.ds((part - 2) * 448 + lo, n)
        if part == 2:
            return wu.at[i, z, rows, :] if stage == 0 else wu.at[:, i, rows, :]
        return wu.at[x, i, rows, :] if stage == 0 else wu.at[i, :, rows, :]

    def step(part, s):
        size = 96 if part < 2 else 448
        stage = s // 2
        along_x = (part % 2 == 0) == (stage == 0)
        me, up, dw = (x, up_x, dn_x) if along_x else (z, up_z, dn_z)
        to_up = dev(up, c, z, y) if along_x else dev(x, c, up, y)
        to_dn = dev(dw, c, z, y) if along_x else dev(x, c, dw, y)
        copies = []
        for way, to in enumerate((to_up, to_dn)):
            if s % 2 == 0:
                ref = slot(part, stage, me, 0, size)
            else:
                ref = slot(part, stage, dw if way == 0 else up, way * (size // 2), size // 2)
            copies.append(
                go(remote(ref, ref, g_send.at[part, s, way], g_recv.at[part, s, way], to))
            )
        return copies

    def done(copies):
        for copy in copies:
            copy.wait_recv()

    dloc.wait()
    dsend.wait_recv()
    d1, d2 = step(0, 0), step(1, 0)
    for k in range(4):
        arrived(wu.at[x, z, pl.ds(640 + 64 * k, 64), :], u_sem.at[k])
        arrived(wu.at[x, z, pl.ds(160 * k, 160), :], w_sem.at[k])
    w1, w2 = step(2, 0), step(3, 0)
    done(d1), done(d2)
    d1, d2 = step(0, 1), step(1, 1)
    done(d1), done(d2)
    d1, d2 = step(0, 2), step(1, 2)
    done(w1), done(w2)
    w1, w2 = step(2, 1), step(3, 1)
    done(d1), done(d2)
    d1, d2 = step(0, 3), step(1, 3)
    done(w1), done(w2)
    w1, w2 = step(2, 2), step(3, 2)

    for k in range(4):
        arrived(ids.at[k], i_recv.at[k])
    for blk in range(4):
        for k in range(4):
            at = slice(blk * 512 + k * 128, blk * 512 + (k + 1) * 128)
            acol[at, :] = jnp.broadcast_to(ids[blk, k : k + 1, :], (128, 128)).T
            scol[at, :] = jnp.broadcast_to(ids[blk, 4 + k : 5 + k, :], (128, 128)).T
    for r in range(2):
        ref = ids.at[2 * r : 2 * r + 2]
        go(remote(ref, hids.at[slot_of[r]], h_send.at[8 + r], h_recv.at[slot_of[r], 4], halo_to[r]))
    for k in range(4):
        arrived(block_rows(0, 0), x_recv.at[1, k])

    done(d1), done(d2)

    def ranks(o):
        blk = ((c + o) % 2) * 2 + (yl + o // 2) % 2
        rows = pl.ds(pl.multiple_of(blk * 512, 512), 512)
        vals = jnp.concatenate(
            [dot(xg[rows, :], dn[k], ((1,), (1,))).astype(BF16) for k in range(4)], axis=1
        )
        first = (c * 2 + yl * 4).astype(F32)
        mine = acol[rows, 0:1] == cols_ref[0:1, :] + first
        kept_vals = jnp.where(mine, vals.astype(F32), 0.0).astype(BF16)
        rpt[own, :, rows] = dot(fold_ref[...], kept_vals, ((1,), (1,))).astype(BF16)
        for k, to in enumerate((sib, mate, diag)):
            ref = rpt.at[own, :, rows]
            remote(ref, ref, r_send.at[k, o], r_recv.at[own, blk], to).start()

    def two_ranks(first):
        def run(o, carry):
            ranks(o)
            return carry

        lax.fori_loop(first, first + 2, run, 0)

    two_ranks(0)
    done(w1), done(w2)
    w1, w2 = step(2, 3), step(3, 3)
    forwards = []
    mblk = 2 * c + 1 - yl
    for k in range(4):
        arrived(block_rows(0, 0), x_recv.at[0, k])
        ref = block_rows(mblk, k)
        forwards.append(go(remote(ref, ref, f_send.at[k], x_recv.at[2, k], sib)))
    done(forwards)
    two_ranks(2)
    done(w1), done(w2)

    lane = lax.broadcasted_iota(jnp.int32, (1, 128), 1)
    lane_adapter = (lane // 16).astype(F32)

    def halo_copies(blk, o):
        r, part = blk // 2, blk % 2
        src = pl.ds(pl.multiple_of(1024 + part * 512, 512), 512)
        dst = pl.ds(pl.multiple_of(part * 512, 512), 512)
        sl = (r + wrap) % 2
        to = dev((x + wrap * r) % 4, c, tz, y3)
        return [
            remote(buf.at[r, src, :], buf.at[sl, dst, :], h_send.at[2 * o + n],
                   h_recv.at[sl, part * 2 + n], to)
            for n, buf in enumerate((kall, vall))
        ]

    def project(o, carry):
        blk = ((c + o) % 2) * 2 + (yl + o // 2) % 2
        for k in range(1, 4):
            src = (own + k) % 4
            arrived(rpt.at[src, :, pl.ds(0, 512)], r_recv.at[src, blk])
        rows = pl.ds(pl.multiple_of(blk * 512, 512), 512)
        total_ranks = rpt[0, :, rows].astype(F32)
        for k in range(1, 4):
            total_ranks = total_ranks + rpt[k, :, rows].astype(F32)
        tiled = dot(total_ranks.T.astype(BF16), tile_ref[...])
        adapters = acol[rows, :]
        for part, col_blocks in enumerate(((0, 1), (2,), (3,))):
            mine = tiled[:, part * 128 : (part + 1) * 128]
            spread = [
                jnp.where(adapters == lane_adapter + 8.0 * n, mine, 0.0).astype(BF16)
                for n in range(8)
            ]
            for cb in col_blocks:
                base = jnp.zeros((512, 256), F32)
                delta = jnp.zeros((512, 256), F32)
                for k in range(4):
                    base = base + dot(xg[rows, k * 640 : (k + 1) * 640], wu[cb, k, 0:640, :])
                    pair = jnp.concatenate([spread[2 * k], spread[2 * k + 1]], axis=1)
                    delta = delta + dot(pair, wu[cb, k, 640:896, :])
                proj = base.astype(BF16).astype(F32) + delta.astype(BF16).astype(F32)
                if cb < 3:
                    scale = lax.rsqrt(jnp.mean(proj * proj, axis=-1, keepdims=True) + 1e-06)
                    gain = gains_ref[0:1, :] if cb < 2 else gains_ref[1:2, :]
                    proj = proj * scale * gain
                val = proj.astype(BF16)
                at = pl.ds(pl.multiple_of(1024 + (blk % 2) * 512, 512), 512)
                if cb < 2:
                    qs[cb, rows, :] = val * BF16(0.0625)
                elif cb == 2:
                    kall[blk // 2, at, :] = val
                else:
                    vall[blk // 2, at, :] = val
        for copy in halo_copies(blk, o):
            copy.start()
        return carry

    lax.fori_loop(0, 4, project, 0)

    for sl in range(2):
        arrived(hids.at[sl], h_recv.at[sl, 4])
    nothing = jnp.where(x * 8 + z * 2 + g == 0, 1.0, 0.0).astype(F32)
    for r in range(2):
        for t in range(8):
            blk, k = (t % 4) // 2, (t % 2) * 2
            if t < 4:
                pair = [hids[r, blk, 4 + k + n : 5 + k + n, :] for n in range(2)]
                if r == 0:
                    pair = [p - nothing * (p + 1.0) for p in pair]
            else:
                pair = [ids[2 * r + blk, 4 + k + n : 5 + k + n, :] for n in range(2)]
            krow[r, t] = jnp.broadcast_to(jnp.concatenate(pair, axis=1), (8, 256))

    ahead = lax.broadcasted_iota(jnp.int32, (256, 256), 0) - lax.broadcasted_iota(
        jnp.int32, (256, 256), 1
    )

    def out_copy(blk):
        src = ob.at[pl.ds(pl.multiple_of(blk * 512, 512), 512), :]
        dst = out_ref.at[:, pl.ds(pl.multiple_of(kv * 512, 512), 512)]
        return src, dst, dev(x, blk // 2, z, g * 2 + blk % 2)

    def attend(n, carry):
        r, i = n // 4, n % 4
        for h in range(2):
            rows = pl.ds(pl.multiple_of(n * 256, 256), 256)
            q = qs[h, rows, :]
            sq = scol[rows, 0:1]
            acc = jnp.zeros((256, 256), F32)
            total = jnp.zeros((256, 128), F32)
            for j in range(5):
                keys = pl.ds(pl.multiple_of((i + j) * 256, 256), 256)
                s = dot(q, kall[r, keys, :], ((1,), (1,)))
                ok = sq == krow[r, i + j, 0:1, :]
                if j == 0:
                    ok = ok & (ahead < 0)
                if j == 4:
                    ok = ok & (ahead >= 0)
                w = jnp.where(ok, jnp.exp(s), 0.0)
                total = total + w[:, 0:128] + w[:, 128:256]
                acc = acc + dot(w.astype(BF16), vall[r, keys, :])
            norm = jnp.sum(total, axis=-1, keepdims=True)
            ob[rows, h * 256 : (h + 1) * 256] = (acc / norm).astype(BF16)

        @pl.when(n % 2 == 1)
        def _():
            blk = n // 2
            src, dst, to = out_copy(blk)

            @pl.when(blk == own)
            def _():
                pltpu.make_async_copy(src, dst, o_recv.at[own]).start()

            @pl.when(blk != own)
            def _():
                remote(src, dst, o_send.at[blk], o_recv.at[own], to).start()

        return carry

    for r in range(2):
        for k in range(4):
            arrived(kall.at[r, pl.ds(0, 512), :], h_recv.at[r, k])
        lax.fori_loop(4 * r, 4 * r + 4, attend, 0)

    for k in range(4):
        arrived(out_ref.at[:, pl.ds(0, 512)], o_recv.at[k])
    for k in range(1, 4):
        blk = (own + k) % 4
        src, dst, to = out_copy(blk)
        remote(src, dst, o_send.at[blk], o_recv.at[own], to).wait_send()
    for o in range(4):
        for k, to in enumerate((sib, mate, diag)):
            ref = rpt.at[own, :, pl.ds(0, 512)]
            remote(ref, ref, r_send.at[k, o], r_recv.at[own, o], to).wait_send()
        blk = ((c + o) % 2) * 2 + (yl + o // 2) % 2
        for copy in halo_copies(blk, o):
            copy.wait_send()
    for yt, send in kept_sends:

        @pl.when(yt != y)
        def _():
            send.wait_send()

    for copy in pending:
        copy.wait_send()


FOLD = np.zeros((48, 768), np.float32)
FOLD[np.arange(768) % 48, np.arange(768)] = 1.0
TILE = np.zeros((48, 384), np.float32)
for _lane in range(384):
    TILE[(_lane // 128) * 16 + _lane % 16, _lane] = 1.0
_c = np.arange(768)
COLS = np.tile(((_c // 192) * 16 + (_c % 192 // 96) * 8 + _c % 96 // 48).astype(np.float32), (8, 1))


def body(
    residual_input,
    input_norm_gain,
    base_projection_weight,
    query_key_gains,
    adapter_down_weight,
    adapter_up_weight,
    row_adapter_index,
    row_sequence_index,
):
    ids = jnp.concatenate(
        [row_adapter_index.reshape(4, 128), row_sequence_index.reshape(4, 128)], axis=0
    ).astype(F32)
    down = jnp.transpose(adapter_down_weight, (0, 2, 1)).reshape(192, WIDTH)
    up = adapter_up_weight.reshape(64, 4096)
    vm = pl.BlockSpec(memory_space=pltpu.VMEM)
    anyspace = pl.BlockSpec(memory_space=pl.ANY)
    dma = pltpu.SemaphoreType.DMA
    return pl.pallas_call(
        kernel,
        out_shape=jax.ShapeDtypeStruct((ROWS, HEADS * HEAD_DIM), BF16),
        in_specs=[vm] * 7 + [anyspace] * 3,
        out_specs=anyspace,
        scratch_shapes=[
            pltpu.VMEM((2048, WIDTH), BF16),
            pltpu.VMEM((4, 4, 896, 256), BF16),
            pltpu.VMEM((4, 192, WIDTH), BF16),
            pltpu.VMEM((4, 48, 2048), BF16),
            pltpu.VMEM((2, 2048, 256), BF16),
            pltpu.VMEM((2, 2048, 256), BF16),
            pltpu.VMEM((2, 2048, 256), BF16),
            pltpu.VMEM((2048, 512), BF16),
            pltpu.VMEM((4, 8, 128), F32),
            pltpu.VMEM((2, 2, 8, 128), F32),
            pltpu.VMEM((2048, 128), F32),
            pltpu.VMEM((2048, 128), F32),
            pltpu.VMEM((2, 8, 8, 256), F32),
            dma((8,)), dma((2,)), dma((4,)), dma((4,)),
            dma((2, 4)), dma((3, 4)), dma((4,)),
            dma((3,)), dma((4,)),
            dma((4, 4, 2)), dma((4, 4, 2)),
            dma((3, 4)), dma((4, 4)),
            dma((10,)), dma((2, 5)),
            dma((4,)), dma((4,)),
        ],
        compiler_params=pltpu.CompilerParams(
            collective_id=0, has_side_effects=True, vmem_limit_bytes=60 << 20
        ),
        name="block",
    )(
        residual_input,
        input_norm_gain.reshape(1, WIDTH),
        query_key_gains,
        ids,
        jnp.asarray(FOLD, BF16),
        jnp.asarray(TILE, BF16),
        jnp.asarray(COLS),
        base_projection_weight,
        down,
        up,
    )


def solution(mesh):
    placed = (
        P(("dp", "adapter"), None),
        P(),
        P("adapter", "dp"),
        P(),
        P("adapter", None, None),
        P("adapter", None, None),
        P(("dp", "adapter"), None),
        P(("dp", "adapter")),
    )
    return jax.shard_map(
        body, mesh=mesh, in_specs=placed, out_specs=P(("dp", "adapter"), None), check_vma=False
    )
```

time: 497 us -> 167 us (0.34)
  the two profiles are of different devices: /device:TPU:3 before, /device:TPU:45 now
where the time goes in v1:
time: 167 us; the launch traced here: 166 us
  Pallas kernels  161 us (96%)
  local copies, waits for them, and re-layouts  4.47 us (3%)
    pallas_call x1, Pallas kernels, body(): pl.pallas_call(kernel, out_shape=jax.ShapeDtypeStruct((ROWS, HEADS * HEAD...  161 us

profile of v1, /device:TPU:45, one launch (start us, length us, event | category | flops | bytes accessed | tf_op | source)
XLA Modules:
  0.0 166.4 jit_solution(14825114475353174904)
XLA Ops:
  0.0 1.3 add_convert_fusion.ids_ref
  1.3 1.3 reshape.15.g_ref
  2.6 160.6 %block.1 = bf16[512,2048]{1,0:T(8,128)(2,1)} custom-call(bf16[512,2560]{1,0:T(8,128)(2,1)} %x_ref.1, f32[1,2560]{1,0:T(1,128)} %reshape.15.g_ref, f32[2,256]{1,0:T(2,128)} %gains_ref.1, f32[8,128]{1,0:T(8,128)} %add_convert_fusion.ids_ref, bf16[48,768]{1,0:T(8,128)(2,1)} %constant.6.clone.fold_ref, bf16[48,384]{1,0:T(8,128)(2,1)} %constant.7.clone.tile_ref, ...), custom_call_target="tpu_custom_call" | custom-call | tf_op jit(solution)/shard_map/block/pallas_call | solution.py:414
  163.3 3.2 %copy.13 = bf16[512,2048]{1,0:T(8,128)(2,1)} copy(bf16[512,2048]{1,0:T(8,128)(2,1)} %block.1) | data formatting | bytes 4194304

commit v2 on v1

v2 whole, which is shorter than its diff:
```python
import jax
import jax.numpy as jnp
import numpy as np
from jax import lax
from jax.experimental import pallas as pl
from jax.experimental.pallas import tpu as pltpu
from jax.sharding import PartitionSpec as P

HEADS = 8
KV_HEADS = 4
HEAD_DIM = 256
ROWS = 512
WIDTH = 2560
BF16 = jnp.bfloat16
F32 = jnp.float32


def dot(a, b, dims=((1,), (0,))):
    return lax.dot_general(a, b, (dims, ((), ())), preferred_element_type=F32)


def kernel(
    x_ref, g_ref, gains_ref, ids_ref, fold_ref, tile_ref, cols_ref, w_ref, d_ref, u_ref,
    out_ref,
    xg, wb, ub, dn, rpt, qs, kall, vall, ob, acc_ref, tot_ref, ids, hids, acol, scol, krow,
    d_send, d_sem, u_send, u_sem, w_send, w_sem, x_send, x_recv, f_send, i_send, i_recv,
    g_send, g_recv, r_send, r_recv, h_send, h_recv, o_send, o_recv,
):
    dp = lax.axis_index("dp")
    ad = lax.axis_index("adapter")
    x, c = dp // 2, dp % 2
    z, y = ad // 4, ad % 4
    g, yl = y // 2, y % 2

    def dev(x_, c_, z_, y_):
        return (x_ * 2 + c_, z_ * 4 + y_)

    def half_of(y_):
        return ((y_ + 1) // 2) % 2

    def remote(src, dst, ssem, rsem, to):
        return pltpu.make_async_remote_copy(
            src_ref=src, dst_ref=dst, send_sem=ssem, recv_sem=rsem,
            device_id=to, device_id_type=pl.DeviceIdType.MESH,
        )

    def arrived(ref, sem):
        pltpu.make_async_copy(ref, ref, sem).wait()

    half = half_of(y)
    kv = c + 2 * half
    ypar = 1 - 2 * yl + y
    sib = dev(x, 1 - c, z, y)
    mate = dev(x, c, z, ypar)
    diag = dev(x, 1 - c, z, ypar)
    xbit = x // 2
    hb = (1 - xbit) * (x % 2) + xbit * c
    up_x, dn_x = (x + 1) % 4, (x + 3) % 4
    up_z, dn_z = (z + 1) % 4, (z + 3) % 4
    y3 = 3 - y
    twin = dev(x, c, z, y3)
    wrap = g * (z // 3)
    tz = (z + g) % 4
    swrap = (1 - g) * ((3 - z) // 3)
    sz = (z + 3 + g) % 4
    halo_to = [dev(x, c, tz, y3), dev((x + wrap) % 4, c, tz, y3)]
    halo_from = [dev((x + 4 - swrap) % 4, c, sz, y3), dev(x, c, sz, y3)]
    slot_of = [wrap, 1 - wrap]
    w_to = []
    for blk in range(2):
        for yt in (hb, 3 - hb):
            w_to.append((blk, yt, (1 - xbit) * c + xbit * blk))
    w_from = [dev(half, c, z, x)] * 2 + [dev(2, half, z, x), dev(3, half, z, x)]
    flip = dev(y, c, z, x)

    barrier = pltpu.get_barrier_semaphore()
    partners = [sib, mate, diag, twin, flip]
    partners += [dev(y, cc, z, yt) for _, yt, cc in w_to] + w_from
    partners += [dev(up_x, c, z, y), dev(dn_x, c, z, y), dev(x, c, up_z, y), dev(x, c, dn_z, y)]
    partners += halo_to + halo_from
    for to in partners:
        pl.semaphore_signal(barrier, inc=1, device_id=to, device_id_type=pl.DeviceIdType.MESH)
    pl.semaphore_wait(barrier, len(partners))

    pending = []

    def go(copy):
        copy.start()
        pending.append(copy)
        return copy

    features = pl.ds(pl.multiple_of(640 * x, 128), 640)
    dsrc = d_ref.at[pl.ds(pl.multiple_of(96 * c, 32), 96), features]
    ddst = dn.at[z, pl.ds(pl.multiple_of(96 * g, 32), 96), features]
    dloc = pltpu.make_async_copy(dsrc, ddst, d_sem.at[0])
    dloc.start()
    dsend = go(remote(dsrc, ddst, d_send.at[0], d_sem.at[1], twin))

    w_copies = []
    for n, (blk, yt, cc) in enumerate(w_to):
        src = w_ref.at[:, blk * 256 : (blk + 1) * 256]
        cb = (1 - xbit) * blk + xbit * x
        dst = wb.at[cb, z, y]
        here = (y == x) & (yt == y) & (cc == c)
        copy = remote(src, dst, w_send.at[n], w_sem.at[cb], dev(y, cc, z, yt))
        w_copies.append((here, copy))

        @pl.when(here)
        def _():
            pltpu.make_async_copy(src, dst, w_sem.at[cb]).start()

        @pl.when(jnp.logical_not(here))
        def _():
            copy.start()

    u_copies = []
    kvx = c + 2 * half_of(x)
    for cb in (2, 3, 0, 1):
        col = kvx * 512 + cb * 256 if cb < 2 else cb * 1024 + kvx * 256
        src = u_ref.at[:, pl.ds(pl.multiple_of(col, 128), 256)]
        dst = ub.at[cb, z, y]
        copy = remote(src, dst, u_send.at[cb], u_sem.at[cb], flip)
        u_copies.append(copy)

        @pl.when(x == y)
        def _():
            pltpu.make_async_copy(src, dst, u_sem.at[cb]).start()

        @pl.when(x != y)
        def _():
            copy.start()

    own = 2 * c + yl
    pltpu.make_async_copy(ids_ref, ids.at[own], i_recv.at[own]).start()
    for k, to in enumerate((sib, mate, diag)):
        go(remote(ids_ref, ids.at[own], i_send.at[k], i_recv.at[own], to))

    def block_rows(blk, k):
        return xg.at[pl.ds(pl.multiple_of(blk * 512 + k * 128, 128), 128), :]

    def to_mate(k):
        ref = block_rows(own, k)
        return remote(ref, ref, x_send.at[0, k], x_recv.at[0, k], mate)

    def forward(k):
        ref = block_rows(2 * c + 1 - yl, k)
        return remote(ref, ref, f_send.at[k], x_recv.at[2, k], sib)

    for k in range(4):
        val = x_ref[k * 128 : (k + 1) * 128, :].astype(F32)
        scale = lax.rsqrt(jnp.mean(val * val, axis=-1, keepdims=True) + 1e-06)
        ref = block_rows(own, k)
        ref[...] = (val * scale * g_ref[...]).astype(BF16)

        @pl.when(c == 0)
        def _():
            to_mate(k).start()

        go(remote(ref, ref, x_send.at[1, k], x_recv.at[1, k], sib))

    def slots(cls, part, stage, i, h):
        out = []
        if cls == 0:
            rows = pl.ds(part * 96, 96) if h is None else pl.ds(part * 96 + h * 48, 48)
            cols_i = pl.ds(pl.multiple_of(i * 640, 128), 640)
            if part == 0:
                out.append(dn.at[z, rows, cols_i] if stage == 0 else dn.at[i, rows, :])
            else:
                out.append(dn.at[i, rows, features] if stage == 0 else dn.at[:, rows, cols_i])
            return out
        cb = (2, 0)[cls - 1] + part
        for buf, size in ((wb, 160), (ub, 64)):
            rows = pl.ds(0, size) if h is None else pl.ds(h * (size // 2), size // 2)
            if part == 0:
                out.append(buf.at[cb, z, i, rows, :] if stage == 0 else buf.at[cb, i, :, rows, :])
            else:
                out.append(buf.at[cb, i, x, rows, :] if stage == 0 else buf.at[cb, :, i, rows, :])
        return out

    def step(cls, s):
        copies = []
        stage = s // 2
        for part in range(2):
            along_x = (part == 0) == (stage == 0)
            me, up, dw = (x, up_x, dn_x) if along_x else (z, up_z, dn_z)
            to_up = dev(up, c, z, y) if along_x else dev(x, c, up, y)
            to_dn = dev(dw, c, z, y) if along_x else dev(x, c, dw, y)
            for way, to in enumerate((to_up, to_dn)):
                if s % 2 == 0:
                    refs = slots(cls, part, stage, me, None)
                else:
                    refs = slots(cls, part, stage, dw if way == 0 else up, way)
                for n, ref in enumerate(refs):
                    at = (2 * cls + part, s, 2 * way + n)
                    copies.append(go(remote(ref, ref, g_send.at[at], g_recv.at[at], to)))
        return copies

    def done(copies):
        for copy in copies:
            copy.wait_recv()

    dloc.wait()
    dsend.wait_recv()
    dd = step(0, 0)
    for cb in (2, 3):
        arrived(wb.at[cb, z, x], w_sem.at[cb])
        arrived(ub.at[cb, z, x], u_sem.at[cb])
    kk = step(1, 0)
    done(dd)
    dd = step(0, 1)
    for cb in (0, 1):
        arrived(wb.at[cb, z, x], w_sem.at[cb])
        arrived(ub.at[cb, z, x], u_sem.at[cb])
    qq = step(2, 0)
    done(dd)
    dd = step(0, 2)
    done(kk)
    kk = step(1, 1)
    done(qq)
    qq = step(2, 1)

    for k in range(4):
        arrived(ids.at[k], i_recv.at[k])
    for blk in range(4):
        for k in range(4):
            at = slice(blk * 512 + k * 128, blk * 512 + (k + 1) * 128)
            acol[at, :] = jnp.broadcast_to(ids[blk, k : k + 1, :], (128, 128)).T
            scol[at, :] = jnp.broadcast_to(ids[blk, 4 + k : 5 + k, :], (128, 128)).T
    for r in range(2):
        ref = ids.at[2 * r : 2 * r + 2]
        go(remote(ref, hids.at[slot_of[r]], h_send.at[8 + r], h_recv.at[slot_of[r], 4], halo_to[r]))
    for k in range(4):
        arrived(block_rows(0, 0), x_recv.at[1, k])

    done(kk)
    done(dd)
    dd = step(0, 3)
    kk = step(1, 2)

    @pl.when(c == 0)
    def _():
        for k in range(4):
            arrived(block_rows(0, 0), x_recv.at[0, k])
            forward(k).start()

    @pl.when(c == 1)
    def _():
        for k in range(4):
            arrived(block_rows(0, 0), x_recv.at[2, k])
            to_mate(k).start()

    done(dd)

    def ranks(blk, carry):
        rows = pl.ds(pl.multiple_of(blk * 512, 512), 512)
        vals = jnp.concatenate(
            [dot(xg[rows, :], dn[k], ((1,), (1,))).astype(BF16) for k in range(4)], axis=1
        )
        first = (c * 2 + half * 4).astype(F32)
        apart = (12 - 8 * half).astype(F32)
        mine = acol[rows, 0:1] == cols_ref[0:1, :] + cols_ref[1:2, :] * apart + first
        kept_vals = jnp.where(mine, vals.astype(F32), 0.0).astype(BF16)
        rpt[own, :, rows] = dot(fold_ref[...], kept_vals, ((1,), (1,))).astype(BF16)
        for k, to in enumerate((sib, mate, diag)):
            ref = rpt.at[own, :, rows]
            remote(ref, ref, r_send.at[k, blk], r_recv.at[own, blk], to).start()
        return carry

    lax.fori_loop(0, 2, ranks, 0)
    done(qq)
    done(kk)
    kk = step(1, 3)
    qq = step(2, 2)

    lane = lax.broadcasted_iota(jnp.int32, (1, 128), 1)
    lane_adapter = (lane // 16).astype(F32)

    def halo_copies(blk):
        r, part = blk // 2, blk % 2
        src = pl.ds(pl.multiple_of(1024 + part * 512, 512), 512)
        dst = pl.ds(pl.multiple_of(part * 512, 512), 512)
        sl = (r + wrap) % 2
        to = dev((x + wrap * r) % 4, c, tz, y3)
        return [
            remote(buf.at[r, src, :], buf.at[sl, dst, :], h_send.at[2 * blk + n],
                   h_recv.at[sl, part * 2 + n], to)
            for n, buf in enumerate((kall, vall))
        ]

    def project(blk, kinds):
        rows = pl.ds(pl.multiple_of(blk * 512, 512), 512)
        total_ranks = rpt[0, :, rows].astype(F32)
        for k in range(1, 4):
            total_ranks = total_ranks + rpt[k, :, rows].astype(F32)
        tiled = dot(total_ranks.T.astype(BF16), tile_ref[...])
        adapters = acol[rows, :]
        for part, col_blocks in kinds:
            mine = tiled[:, part * 128 : (part + 1) * 128]
            spread = jnp.concatenate(
                [
                    jnp.where(adapters == lane_adapter + 8.0 * n, mine, 0.0).astype(BF16)
                    for n in range(8)
                ],
                axis=1,
            )
            for cb in col_blocks:
                base = dot(xg[rows, :], wb[cb].reshape(WIDTH, 256))
                delta = dot(spread, ub[cb].reshape(1024, 256))
                proj = base.astype(BF16).astype(F32) + delta.astype(BF16).astype(F32)
                if cb < 3:
                    scale = lax.rsqrt(jnp.mean(proj * proj, axis=-1, keepdims=True) + 1e-06)
                    gain = gains_ref[0:1, :] if cb < 2 else gains_ref[1:2, :]
                    proj = proj * scale * gain
                val = proj.astype(BF16)
                at = pl.ds(pl.multiple_of(1024 + (blk % 2) * 512, 512), 512)
                if cb < 2:
                    qs[cb, rows, :] = val * BF16(0.0625)
                elif cb == 2:
                    kall[blk // 2, at, :] = val
                else:
                    vall[blk // 2, at, :] = val

    def project_kv(n, carry):
        blk = n // 2 * 2 + 1 - n % 2
        for k in range(1, 4):
            src = (own + k) % 4
            arrived(rpt.at[src, :, pl.ds(0, 512)], r_recv.at[src, blk])
        project(blk, ((1, (2,)), (2, (3,))))
        for copy in halo_copies(blk):
            copy.start()
        return carry

    def project_q(blk, carry):
        project(blk, ((0, (0, 1)),))
        return carry

    done(kk)
    lax.fori_loop(0, 2, project_kv, 0)
    done(qq)
    qq = step(2, 3)

    @pl.when(c == 1)
    def _():
        for k in range(4):
            arrived(block_rows(0, 0), x_recv.at[0, k])
            forward(k).start()

    @pl.when(c == 0)
    def _():
        for k in range(4):
            arrived(block_rows(0, 0), x_recv.at[2, k])

    lax.fori_loop(2, 4, ranks, 0)
    done(qq)
    lax.fori_loop(0, 2, project_q, 0)
    lax.fori_loop(2, 4, project_kv, 0)
    lax.fori_loop(2, 4, project_q, 0)

    for sl in range(2):
        arrived(hids.at[sl], h_recv.at[sl, 4])
    nothing = jnp.where(x * 8 + z * 2 + g == 0, 1.0, 0.0).astype(F32)
    for r in range(2):
        for t in range(8):
            blk, k = (t % 4) // 2, (t % 2) * 2
            if t < 4:
                pair = [hids[r, blk, 4 + k + n : 5 + k + n, :] for n in range(2)]
                if r == 0:
                    pair = [p - nothing * (p + 1.0) for p in pair]
            else:
                pair = [ids[2 * r + blk, 4 + k + n : 5 + k + n, :] for n in range(2)]
            krow[r, t] = jnp.broadcast_to(jnp.concatenate(pair, axis=1), (8, 256))

    ahead = lax.broadcasted_iota(jnp.int32, (256, 256), 0) - lax.broadcasted_iota(
        jnp.int32, (256, 256), 1
    )

    def attend(r, i, h, tiles, acc, total):
        rows = slice(r * 1024 + i * 256, r * 1024 + (i + 1) * 256)
        q = qs[h, rows, :]
        sq = scol[rows, 0:1]
        for t in tiles:
            keys = slice(t * 256, (t + 1) * 256)
            s = dot(q, kall[r, keys, :], ((1,), (1,)))
            ok = sq == krow[r, t, 0:1, :]
            if t == i:
                ok = ok & (ahead < 0)
            if t == i + 4:
                ok = ok & (ahead >= 0)
            w = jnp.where(ok, jnp.exp(s), 0.0)
            more = w[:, 0:128] + w[:, 128:256]
            part = dot(w.astype(BF16), vall[r, keys, :])
            total = more if total is None else total + more
            acc = part if acc is None else acc + part
        return acc, total

    def attend_own(r):
        for i in range(4):
            at = slice(i * 256, (i + 1) * 256)

            def head(h, carry):
                acc, total = attend(r, i, h, range(4, 5 + i), None, None)
                acc_ref[h, at, :] = acc
                tot_ref[h, at, :] = total
                return carry

            lax.fori_loop(0, 2, head, 0)

    def out_copy(blk):
        src = ob.at[:, blk * 512 : (blk + 1) * 512, :]
        refs = []
        for h in range(2):
            dst = out_ref.at[:, pl.ds(pl.multiple_of(kv * 512 + h * 256, 256), 256)]
            refs.append((src.at[h], dst))
        return refs, dev(x, blk // 2, z, g * 2 + blk % 2)

    def attend_halo(r, part):
        for i in (2 * part + 1, 2 * part):
            at = slice(i * 256, (i + 1) * 256)
            rows = slice(r * 1024 + i * 256, r * 1024 + (i + 1) * 256)

            def head(h, carry):
                acc, total = attend(r, i, h, range(i, 4), acc_ref[h, at, :], tot_ref[h, at, :])
                norm = jnp.sum(total, axis=-1, keepdims=True)
                ob[h, rows, :] = (acc / norm).astype(BF16)
                return carry

            lax.fori_loop(0, 2, head, 0)
        blk = 2 * r + part
        refs, to = out_copy(blk)

        @pl.when(blk == own)
        def _():
            for h, (src, dst) in enumerate(refs):
                pltpu.make_async_copy(src, dst, o_recv.at[own, h]).start()

        @pl.when(blk != own)
        def _():
            for h, (src, dst) in enumerate(refs):
                remote(src, dst, o_send.at[blk, h], o_recv.at[own, h], to).start()

    for r in range(2):
        attend_own(r)
        for part in (1, 0):
            for n in range(2):
                arrived(kall.at[r, pl.ds(0, 512), :], h_recv.at[r, 2 * part + n])
            attend_halo(r, part)

    for k in range(4):
        for h in range(2):
            arrived(out_ref.at[:, pl.ds(0, 256)], o_recv.at[k, h])
    for blk in range(4):
        refs, to = out_copy(blk)

        @pl.when(blk != own)
        def _():
            for h, (src, dst) in enumerate(refs):
                remote(src, dst, o_send.at[blk, h], o_recv.at[own, h], to).wait_send()

        for k, to in enumerate((sib, mate, diag)):
            ref = rpt.at[own, :, pl.ds(0, 512)]
            remote(ref, ref, r_send.at[k, blk], r_recv.at[own, blk], to).wait_send()
        for copy in halo_copies(blk):
            copy.wait_send()
    for k in range(4):
        to_mate(k).wait_send()
        forward(k).wait_send()
    for here, copy in w_copies:

        @pl.when(jnp.logical_not(here))
        def _():
            copy.wait_send()

    for copy in u_copies:

        @pl.when(x != y)
        def _():
            copy.wait_send()

    for copy in pending:
        copy.wait_send()


FOLD = np.zeros((48, 768), np.float32)
FOLD[np.arange(768) % 48, np.arange(768)] = 1.0
TILE = np.zeros((48, 384), np.float32)
for _lane in range(384):
    TILE[(_lane // 128) * 16 + _lane % 16, _lane] = 1.0
_c = np.arange(768)
COLS = np.zeros((8, 768), np.float32)
COLS[0] = (_c // 192) * 16 + _c % 96 // 48
COLS[1] = _c % 192 // 96


def body(
    residual_input,
    input_norm_gain,
    base_projection_weight,
    query_key_gains,
    adapter_down_weight,
    adapter_up_weight,
    row_adapter_index,
    row_sequence_index,
):
    ids = jnp.concatenate(
        [row_adapter_index.reshape(4, 128), row_sequence_index.reshape(4, 128)], axis=0
    ).astype(F32)
    down = jnp.transpose(adapter_down_weight, (0, 2, 1)).reshape(192, WIDTH)
    up = adapter_up_weight.reshape(64, 4096)
    vm = pl.BlockSpec(memory_space=pltpu.VMEM)
    anyspace = pl.BlockSpec(memory_space=pl.ANY)
    dma = pltpu.SemaphoreType.DMA
    return pl.pallas_call(
        kernel,
        out_shape=jax.ShapeDtypeStruct((ROWS, HEADS * HEAD_DIM), BF16),
        in_specs=[vm] * 7 + [anyspace] * 3,
        out_specs=anyspace,
        scratch_shapes=[
            pltpu.VMEM((2048, WIDTH), BF16),
            pltpu.VMEM((4, 4, 4, 160, 256), BF16),
            pltpu.VMEM((4, 4, 4, 64, 256), BF16),
            pltpu.VMEM((4, 192, WIDTH), BF16),
            pltpu.VMEM((4, 48, 2048), BF16),
            pltpu.VMEM((2, 2048, 256), BF16),
            pltpu.VMEM((2, 2048, 256), BF16),
            pltpu.VMEM((2, 2048, 256), BF16),
            pltpu.VMEM((2, 2048, 256), BF16),
            pltpu.VMEM((2, 1024, 256), F32),
            pltpu.VMEM((2, 1024, 128), F32),
            pltpu.VMEM((4, 8, 128), F32),
            pltpu.VMEM((2, 2, 8, 128), F32),
            pltpu.VMEM((2048, 128), F32),
            pltpu.VMEM((2048, 128), F32),
            pltpu.VMEM((2, 8, 8, 256), F32),
            dma((1,)), dma((2,)), dma((4,)), dma((4,)), dma((4,)), dma((4,)),
            dma((2, 4)), dma((3, 4)), dma((4,)),
            dma((3,)), dma((4,)),
            dma((6, 4, 4)), dma((6, 4, 4)),
            dma((3, 4)), dma((4, 4)),
            dma((10,)), dma((2, 5)),
            dma((4, 2)), dma((4, 2)),
        ],
        compiler_params=pltpu.CompilerParams(
            collective_id=0, has_side_effects=True, vmem_limit_bytes=60 << 20
        ),
        name="block",
    )(
        residual_input,
        input_norm_gain.reshape(1, WIDTH),
        query_key_gains,
        ids,
        jnp.asarray(FOLD, BF16),
        jnp.asarray(TILE, BF16),
        jnp.asarray(COLS),
        base_projection_weight,
        down,
        up,
    )


def solution(mesh):
    placed = (
        P(("dp", "adapter"), None),
        P(),
        P("adapter", "dp"),
        P(),
        P("adapter", None, None),
        P("adapter", None, None),
        P(("dp", "adapter"), None),
        P(("dp", "adapter")),
    )
    return jax.shard_map(
        body, mesh=mesh, in_specs=placed, out_specs=P(("dp", "adapter"), None), check_vma=False
    )
```

time: 167 us -> 201 us (1.20)
  the two profiles are of different devices: /device:TPU:45 before, /device:TPU:3 now
where the time goes in v2:
time: 201 us; the launch traced here: 198 us
  Pallas kernels  192 us (96%)
  local copies, waits for them, and re-layouts  4.47 us (2%)
    pallas_call x1, Pallas kernels, body(): pl.pallas_call(kernel, out_shape=jax.ShapeDtypeStruct((ROWS, HEADS * HEAD...  192 us

profile of v2, /device:TPU:3, one launch (start us, length us, event | category | flops | bytes accessed | tf_op | source)
XLA Modules:
  0.0 198.3 jit_solution(5197238077569976389)
XLA Ops:
  0.0 1.3 add_convert_fusion.ids_ref
  1.3 1.3 reshape.15.g_ref
  2.6 192.5 %block.1 = bf16[512,2048]{1,0:T(8,128)(2,1)} custom-call(bf16[512,2560]{1,0:T(8,128)(2,1)} %x_ref.1, f32[1,2560]{1,0:T(1,128)} %reshape.15.g_ref, f32[2,256]{1,0:T(2,128)} %gains_ref.1, f32[8,128]{1,0:T(8,128)} %add_convert_fusion.ids_ref, bf16[48,768]{1,0:T(8,128)(2,1)} %constant.6.clone.fold_ref, bf16[48,384]{1,0:T(8,128)(2,1)} %constant.7.clone.tile_ref, ...), custom_call_target="tpu_custom_call" | custom-call | tf_op jit(solution)/shard_map/block/pallas_call | solution.py:512
  195.1 3.2 %copy.13 = bf16[512,2048]{1,0:T(8,128)(2,1)} copy(bf16[512,2048]{1,0:T(8,128)(2,1)} %block.1) | data formatting | bytes 4194304

commit v3 on v1

--- a/solution.py
+++ b/solution.py
@@ -20,9 +20,9 @@
 
 
 def kernel(
-    x_ref, g_ref, gains_ref, ids_ref, fold_ref, tile_ref, cols_ref, w_ref, d_ref, u_ref,
+    x_ref, g_ref, gains_ref, aid_ref, sid_ref, fold_ref, tile_ref, cols_ref, w_ref, d_ref, u_ref,
     out_ref,
-    xg, wu, dn, rpt, qs, kall, vall, ob, ids, hids, acol, scol, krow,
+    xg, wu, dn, rpt, qs, kall, vall, ob, acc_ref, tot_ref, ids, hids, acol, scol, krow,
     sh_send, d_sem, u_sem, w_sem, x_send, x_recv, f_send, i_send, i_recv,
     g_send, g_recv, r_send, r_recv, h_send, h_recv, o_send, o_recv,
 ):
@@ -121,17 +121,16 @@
         go(remote(other, wu.at[px, z, wrows, :], sh_send.at[6 + k], w_sem.at[y], dev(px, pc, z, yt)))
 
     own = 2 * c + yl
-    iloc = pltpu.make_async_copy(ids_ref, ids.at[own], i_recv.at[own])
-    iloc.start()
-    for k, to in enumerate((sib, mate, diag)):
-        go(remote(ids_ref, ids.at[own], i_send.at[k], i_recv.at[own], to))
+    ids[own] = jnp.concatenate([aid_ref[...], sid_ref[...]], axis=0).astype(F32)
     for k in range(4):
         val = x_ref[k * 128 : (k + 1) * 128, :].astype(F32)
         scale = lax.rsqrt(jnp.mean(val * val, axis=-1, keepdims=True) + 1e-06)
         rows = pl.ds(pl.multiple_of(own * 512 + k * 128, 128), 128)
-        xg[rows, :] = (val * scale * g_ref[...]).astype(BF16)
-        go(remote(xg.at[rows, :], xg.at[rows, :], x_send.at[0, k], x_recv.at[0, k], mate))
+        xg[rows, :] = (val * scale * g_ref[...].reshape(1, WIDTH)).astype(BF16)
         go(remote(xg.at[rows, :], xg.at[rows, :], x_send.at[1, k], x_recv.at[1, k], sib))
+
+    for k, to in enumerate((sib, mate, diag)):
+        go(remote(ids.at[own], ids.at[own], i_send.at[k], i_recv.at[own], to))
 
     def block_rows(blk, k):
         return xg.at[pl.ds(pl.multiple_of(blk * 512 + k * 128, 128), 128), :]
@@ -178,6 +177,9 @@
         arrived(wu.at[x, z, pl.ds(640 + 64 * k, 64), :], u_sem.at[k])
         arrived(wu.at[x, z, pl.ds(160 * k, 160), :], w_sem.at[k])
     w1, w2 = step(2, 0), step(3, 0)
+    for k in range(4):
+        ref = block_rows(own, k)
+        go(remote(ref, ref, x_send.at[0, k], x_recv.at[0, k], mate))
     done(d1), done(d2)
     d1, d2 = step(0, 1), step(1, 1)
     done(d1), done(d2)
@@ -189,8 +191,8 @@
     done(w1), done(w2)
     w1, w2 = step(2, 2), step(3, 2)
 
-    for k in range(4):
-        arrived(ids.at[k], i_recv.at[k])
+    for k in range(1, 4):
+        arrived(ids.at[0], i_recv.at[(own + k) % 4])
     for blk in range(4):
         for k in range(4):
             at = slice(blk * 512 + k * 128, blk * 512 + (k + 1) * 128)
@@ -253,18 +255,14 @@
             for n, buf in enumerate((kall, vall))
         ]
 
-    def project(o, carry):
-        blk = ((c + o) % 2) * 2 + (yl + o // 2) % 2
-        for k in range(1, 4):
-            src = (own + k) % 4
-            arrived(rpt.at[src, :, pl.ds(0, 512)], r_recv.at[src, blk])
+    def project(blk, kinds):
         rows = pl.ds(pl.multiple_of(blk * 512, 512), 512)
         total_ranks = rpt[0, :, rows].astype(F32)
         for k in range(1, 4):
             total_ranks = total_ranks + rpt[k, :, rows].astype(F32)
         tiled = dot(total_ranks.T.astype(BF16), tile_ref[...])
         adapters = acol[rows, :]
-        for part, col_blocks in enumerate(((0, 1), (2,), (3,))):
+        for part, col_blocks in kinds:
             mine = tiled[:, part * 128 : (part + 1) * 128]
             spread = [
                 jnp.where(adapters == lane_adapter + 8.0 * n, mine, 0.0).astype(BF16)
@@ -290,11 +288,23 @@
                     kall[blk // 2, at, :] = val
                 else:
                     vall[blk // 2, at, :] = val
+
+    def project_kv(o, carry):
+        blk = o // 2 * 2 + 1 - o % 2
+        for k in range(1, 4):
+            src = (own + k) % 4
+            arrived(rpt.at[src, :, pl.ds(0, 512)], r_recv.at[src, blk])
+        project(blk, ((1, (2,)), (2, (3,))))
         for copy in halo_copies(blk, o):
             copy.start()
         return carry
 
-    lax.fori_loop(0, 4, project, 0)
+    def project_q(blk, carry):
+        project(blk, ((0, (0, 1)),))
+        return carry
+
+    lax.fori_loop(0, 4, project_kv, 0)
+    lax.fori_loop(0, 4, project_q, 0)
 
     for sl in range(2):
         arrived(hids.at[sl], h_recv.at[sl, 4])
@@ -314,64 +324,88 @@
         jnp.int32, (256, 256), 1
     )
 
-    def out_copy(blk):
-        src = ob.at[pl.ds(pl.multiple_of(blk * 512, 512), 512), :]
-        dst = out_ref.at[:, pl.ds(pl.multiple_of(kv * 512, 512), 512)]
+    def attend(r, i, h, tiles, acc, total):
+        rows = slice(r * 1024 + i * 256, r * 1024 + (i + 1) * 256)
+        q = qs[h, rows, :]
+        sq = scol[rows, 0:1]
+        for t in tiles:
+            keys = slice(t * 256, (t + 1) * 256)
+            s = dot(q, kall[r, keys, :], ((1,), (1,)))
+            ok = sq == krow[r, t, 0:1, :]
+            if t == i:
+                ok = ok & (ahead < 0)
+            if t == i + 4:
+                ok = ok & (ahead >= 0)
+            w = jnp.where(ok, jnp.exp(s), 0.0)
+            more = w[:, 0:128] + w[:, 128:256]
+            part = dot(w.astype(BF16), vall[r, keys, :])
+            total = more if total is None else total + more
+            acc = part if acc is None else acc + part
+        return acc, total
+
+    def attend_own(r):
+        for i in range(4):
+            at = slice(i * 256, (i + 1) * 256)
+
+            def head(h, carry):
+                acc, total = attend(r, i, h, range(4, 5 + i), None, None)
+                acc_ref[h, at, :] = acc
+                tot_ref[h, at, :] = total
+                return carry
+
+            lax.fori_loop(0, 2, head, 0)
+
+    def out_copy(blk, m):
+        src = ob.at[pl.ds(blk * 512 + m * 256, 256), :]
+        dst = out_ref.at[m * 256 : (m + 1) * 256, pl.ds(pl.multiple_of(kv * 512, 512), 512)]
         return src, dst, dev(x, blk // 2, z, g * 2 + blk % 2)
 
-    def attend(n, carry):
-        r, i = n // 4, n % 4
-        for h in range(2):
-            rows = pl.ds(pl.multiple_of(n * 256, 256), 256)
-            q = qs[h, rows, :]
-            sq = scol[rows, 0:1]
-            acc = jnp.zeros((256, 256), F32)
-            total = jnp.zeros((256, 128), F32)
-            for j in range(5):
-                keys = pl.ds(pl.multiple_of((i + j) * 256, 256), 256)
-                s = dot(q, kall[r, keys, :], ((1,), (1,)))
-                ok = sq == krow[r, i + j, 0:1, :]
-                if j == 0:
-                    ok = ok & (ahead < 0)
-                if j == 4:
-                    ok = ok & (ahead >= 0)
-                w = jnp.where(ok, jnp.exp(s), 0.0)
-                total = total + w[:, 0:128] + w[:, 128:256]
-                acc = acc + dot(w.astype(BF16), vall[r, keys, :])
-            norm = jnp.sum(total, axis=-1, keepdims=True)
-            ob[rows, h * 256 : (h + 1) * 256] = (acc / norm).astype(BF16)
-
-        @pl.when(n % 2 == 1)
-        def _():
-            blk = n // 2
-            src, dst, to = out_copy(blk)
+    def attend_halo(r, part):
+        for i in (2 * part + 1, 2 * part):
+            at = slice(i * 256, (i + 1) * 256)
+            rows = slice(r * 1024 + i * 256, r * 1024 + (i + 1) * 256)
+
+            def head(h, carry):
+                acc, total = attend(r, i, h, range(i, 4), acc_ref[h, at, :], tot_ref[h, at, :])
+                norm = jnp.sum(total, axis=-1, keepdims=True)
+                ob[rows, pl.ds(pl.multiple_of(h * 256, 256), 256)] = (acc / norm).astype(BF16)
+                return carry
+
+            lax.fori_loop(0, 2, head, 0)
+            blk, m = 2 * r + part, i % 2
+            src, dst, to = out_copy(blk, m)
 
             @pl.when(blk == own)
             def _():
-                pltpu.make_async_copy(src, dst, o_recv.at[own]).start()
+                pltpu.make_async_copy(src, dst, o_recv.at[own, m]).start()
 
             @pl.when(blk != own)
             def _():
-                remote(src, dst, o_send.at[blk], o_recv.at[own], to).start()
-
-        return carry
+                remote(src, dst, o_send.at[blk, m], o_recv.at[own, m], to).start()
 
     for r in range(2):
-        for k in range(4):
-            arrived(kall.at[r, pl.ds(0, 512), :], h_recv.at[r, k])
-        lax.fori_loop(4 * r, 4 * r + 4, attend, 0)
+        attend_own(r)
+        for part in (1, 0):
+            for n in range(2):
+                arrived(kall.at[r, pl.ds(0, 512), :], h_recv.at[r, 2 * part + n])
+            attend_halo(r, part)
 
     for k in range(4):
-        arrived(out_ref.at[:, pl.ds(0, 512)], o_recv.at[k])
-    for k in range(1, 4):
-        blk = (own + k) % 4
-        src, dst, to = out_copy(blk)
-        remote(src, dst, o_send.at[blk], o_recv.at[own], to).wait_send()
+        for m in range(2):
+            arrived(out_ref.at[0:256, pl.ds(0, 512)], o_recv.at[k, m])
+    for blk in range(4):
+
+        @pl.when(blk != own)
+        def _():
+            for m in range(2):
+                src, dst, to = out_copy(blk, m)
+                remote(src, dst, o_send.at[blk, m], o_recv.at[own, m], to).wait_send()
+
     for o in range(4):
         for k, to in enumerate((sib, mate, diag)):
             ref = rpt.at[own, :, pl.ds(0, 512)]
             remote(ref, ref, r_send.at[k, o], r_recv.at[own, o], to).wait_send()
-        blk = ((c + o) % 2) * 2 + (yl + o // 2) % 2
+        blk = o // 2 * 2 + 1 - o % 2
         for copy in halo_copies(blk, o):
             copy.wait_send()
     for yt, send in kept_sends:
@@ -403,9 +437,6 @@
     row_adapter_index,
     row_sequence_index,
 ):
-    ids = jnp.concatenate(
-        [row_adapter_index.reshape(4, 128), row_sequence_index.reshape(4, 128)], axis=0
-    ).astype(F32)
     down = jnp.transpose(adapter_down_weight, (0, 2, 1)).reshape(192, WIDTH)
     up = adapter_up_weight.reshape(64, 4096)
     vm = pl.BlockSpec(memory_space=pltpu.VMEM)
@@ -414,7 +445,7 @@
     return pl.pallas_call(
         kernel,
         out_shape=jax.ShapeDtypeStruct((ROWS, HEADS * HEAD_DIM), BF16),
-        in_specs=[vm] * 7 + [anyspace] * 3,
+        in_specs=[vm] * 8 + [anyspace] * 3,
         out_specs=anyspace,
         scratch_shapes=[
             pltpu.VMEM((2048, WIDTH), BF16),
@@ -425,6 +456,8 @@
             pltpu.VMEM((2, 2048, 256), BF16),
             pltpu.VMEM((2, 2048, 256), BF16),
             pltpu.VMEM((2048, 512), BF16),
+            pltpu.VMEM((2, 1024, 256), F32),
+            pltpu.VMEM((2, 1024, 128), F32),
             pltpu.VMEM((4, 8, 128), F32),
             pltpu.VMEM((2, 2, 8, 128), F32),
             pltpu.VMEM((2048, 128), F32),
@@ -436,7 +469,7 @@
             dma((4, 4, 2)), dma((4, 4, 2)),
             dma((3, 4)), dma((4, 4)),
             dma((10,)), dma((2, 5)),
-            dma((4,)), dma((4,)),
+            dma((4, 2)), dma((4, 2)),
         ],
         compiler_params=pltpu.CompilerParams(
             collective_id=0, has_side_effects=True, vmem_limit_bytes=60 << 20
@@ -444,9 +477,10 @@
         name="block",
     )(
         residual_input,
-        input_norm_gain.reshape(1, WIDTH),
+        input_norm_gain,
         query_key_gains,
-        ids,
+        row_adapter_index.reshape(4, 128),
+        row_sequence_index.reshape(4, 128),
         jnp.asarray(FOLD, BF16),
         jnp.asarray(TILE, BF16),
         jnp.asarray(COLS),

time: 167 us -> 155 us (0.928)
  the two profiles are of different devices: /device:TPU:45 before, /device:TPU:3 now
where the time goes in v3:
time: 155 us; the launch traced here: 153 us
  Pallas kernels  150 us (97%)
  local copies, waits for them, and re-layouts  3.16 us (2%)
    pallas_call x1, Pallas kernels, body(): pl.pallas_call(kernel, out_shape=jax.ShapeDtypeStruct((ROWS, HEADS * HEAD...  150 us
    unnamed x1, local copies, waits for them, and re-layouts  3.16 us

profile of v3, /device:TPU:3, one launch (start us, length us, event | category | flops | bytes accessed | tf_op | source)
XLA Modules:
  0.0 153.2 jit_solution(14246722057404535707)
XLA Ops:
  0.0 150.1 %block.1 = bf16[512,2048]{1,0:T(8,128)(2,1)} custom-call(bf16[512,2560]{1,0:T(8,128)(2,1)} %x_ref.1, f32[2560]{0:T(1024)} %g_ref.1, f32[2,256]{1,0:T(2,128)} %gains_ref.1, s32[4,128]{1,0:T(4,128)} %bitcast.8, s32[4,128]{1,0:T(4,128)} %bitcast.9, bf16[48,768]{1,0:T(8,128)(2,1)} %constant.6.clone.fold_ref, bf16[48,384]{1,0:T(8,128)(2,1)} %constant.7.clone.tile_ref, ...), custom_call_target="tpu_custom_call" | custom-call | tf_op jit(solution)/shard_map/block/pallas_call | solution.py:445
  150.1 3.2 %copy.13 = bf16[512,2048]{1,0:T(8,128)(2,1)} copy(bf16[512,2048]{1,0:T(8,128)(2,1)} %block.1) | data formatting | bytes 4194304

commit v4 on v3

--- a/solution.py
+++ b/solution.py
@@ -227,17 +227,18 @@
 
         lax.fori_loop(first, first + 2, run, 0)
 
-    two_ranks(0)
     done(w1), done(w2)
     w1, w2 = step(2, 3), step(3, 3)
+    two_ranks(0)
     forwards = []
     mblk = 2 * c + 1 - yl
     for k in range(4):
         arrived(block_rows(0, 0), x_recv.at[0, k])
         ref = block_rows(mblk, k)
         forwards.append(go(remote(ref, ref, f_send.at[k], x_recv.at[2, k], sib)))
+    ranks(2)
     done(forwards)
-    two_ranks(2)
+    ranks(3)
     done(w1), done(w2)
 
     lane = lax.broadcasted_iota(jnp.int32, (1, 128), 1)
@@ -349,8 +350,8 @@
 
             def head(h, carry):
                 acc, total = attend(r, i, h, range(4, 5 + i), None, None)
-                acc_ref[h, at, :] = acc
-                tot_ref[h, at, :] = total
+                acc_ref[r, h, at, :] = acc
+                tot_ref[r, h, at, :] = total
                 return carry
 
             lax.fori_loop(0, 2, head, 0)
@@ -366,7 +367,7 @@
             rows = slice(r * 1024 + i * 256, r * 1024 + (i + 1) * 256)
 
             def head(h, carry):
-                acc, total = attend(r, i, h, range(i, 4), acc_ref[h, at, :], tot_ref[h, at, :])
+                acc, total = attend(r, i, h, range(i, 4), acc_ref[r, h, at, :], tot_ref[r, h, at, :])
                 norm = jnp.sum(total, axis=-1, keepdims=True)
                 ob[rows, pl.ds(pl.multiple_of(h * 256, 256), 256)] = (acc / norm).astype(BF16)
                 return carry
@@ -383,8 +384,9 @@
             def _():
                 remote(src, dst, o_send.at[blk, m], o_recv.at[own, m], to).start()
 
+    attend_own(0)
+    attend_own(1)
     for r in range(2):
-        attend_own(r)
         for part in (1, 0):
             for n in range(2):
                 arrived(kall.at[r, pl.ds(0, 512), :], h_recv.at[r, 2 * part + n])
@@ -456,8 +458,8 @@
             pltpu.VMEM((2, 2048, 256), BF16),
             pltpu.VMEM((2, 2048, 256), BF16),
             pltpu.VMEM((2048, 512), BF16),
-            pltpu.VMEM((2, 1024, 256), F32),
-            pltpu.VMEM((2, 1024, 128), F32),
+            pltpu.VMEM((2, 2, 1024, 256), F32),
+            pltpu.VMEM((2, 2, 1024, 128), F32),
             pltpu.VMEM((4, 8, 128), F32),
             pltpu.VMEM((2, 2, 8, 128), F32),
             pltpu.VMEM((2048, 128), F32),

time: 155 us -> 152 us (0.981)
  Pallas kernels: 150 us -> 148 us
    pallas_call x1, Pallas kernels: 150 us -> 148 us  [body(): pl.pallas_call(kernel, out_shape=jax.ShapeDtypeStruct((ROWS, HEADS * HEAD...]
where the time goes in v4:
time: 152 us
  Pallas kernels  148 us (97%)
  local copies, waits for them, and re-layouts  3.16 us (2%)
    pallas_call x1, Pallas kernels, body(): pl.pallas_call(kernel, out_shape=jax.ShapeDtypeStruct((ROWS, HEADS * HEAD...  148 us
    unnamed x1, local copies, waits for them, and re-layouts  3.16 us

profile of v4, /device:TPU:3, one launch (start us, length us, event | category | flops | bytes accessed | tf_op | source)
XLA Modules:
  0.0 151.5 jit_solution(3820701944859525827)
XLA Ops:
  0.0 148.4 %block.1 = bf16[512,2048]{1,0:T(8,128)(2,1)} custom-call(bf16[512,2560]{1,0:T(8,128)(2,1)} %x_ref.1, f32[2560]{0:T(1024)} %g_ref.1, f32[2,256]{1,0:T(2,128)} %gains_ref.1, s32[4,128]{1,0:T(4,128)} %bitcast.8, s32[4,128]{1,0:T(4,128)} %bitcast.9, bf16[48,768]{1,0:T(8,128)(2,1)} %constant.6.clone.fold_ref, bf16[48,384]{1,0:T(8,128)(2,1)} %constant.7.clone.tile_ref, ...), custom_call_target="tpu_custom_call" | custom-call | tf_op jit(solution)/shard_map/block/pallas_call | solution.py:447
  148.4 3.2 %copy.13 = bf16[512,2048]{1,0:T(8,128)(2,1)} copy(bf16[512,2048]{1,0:T(8,128)(2,1)} %block.1) | data formatting | bytes 4194304
